TPU v7x, 256 devices: a whole 4x4x8 slice. The times are simulated.
256 devices in a mesh: rows: 16 (over x, z_hi, core), params: 16 (over z_lo, y).
Axes of the slice: x: 4, y: 4, z: 8 (z_hi: 2, z_lo: 4; z = z_hi * 4 + z_lo), core: 2. Of those that a mesh axis runs over, the one named last changes fastest.
Arguments:
- jacobian: bfloat16 [32768, 12288], P('rows', 'params'), may hold values from -0.0546875 to 0.0546875
- pattern: int32 [256, 96], P('rows', 'params'), may hold values from 0 to 1, as said below
- row_class: int32 [32768], P('rows'), may hold values from 0 to 15
- class_weight: float32 [16], replicated, may hold values from 0.1 to 10
- probes: bfloat16 [32, 12288], P(None, 'params'), may hold values from -6 to 6
Outputs:
- basis: bfloat16 [32, 12288], P(None, 'params')
Inputs may be any that keep to these rules, and one draw needn't show every extreme that they name: `pattern`: 1 marks a nonzero block of the Jacobian, 0 a zero block.
All inputs are finite; a program needn't handle non-finite values.
Results may differ from a plain program's by a relative error of at most 0.0075.
Values may be sent and summed in bfloat16 or wider, within the bound.
A program may use at most 64 MiB of HBM per device.

v0:
```python
import math
import jax
import jax.numpy as jnp
from jax import lax
from jax.sharding import PartitionSpec as P

P_SIZE = 12288
ITERS = 4


def local(jacobian, pattern, row_class, class_weight, probes):
    block = jacobian.shape[0] // pattern.shape[0]
    mask_full = jnp.repeat(jnp.repeat(pattern, block, axis=0), block, axis=1)
    masked = jacobian * mask_full.astype(jnp.bfloat16)
    classes = jnp.arange(class_weight.shape[0], dtype=jnp.int32)
    onehot = (row_class[None, :] == classes[:, None]).astype(jnp.float32)
    weight = jnp.sum(onehot * class_weight[:, None], axis=0)
    scale = math.sqrt(P_SIZE)
    basis = probes
    for step in range(ITERS):
        zpart = lax.dot_general(
            basis, masked, (((1,), (1,)), ((), ())), preferred_element_type=jnp.float32
        )
        ztotal = lax.psum(zpart, "params")
        weighted = (ztotal * weight[None, :]).astype(jnp.bfloat16)
        ypart = jnp.dot(weighted, masked, preferred_element_type=jnp.float32)
        ytotal = lax.psum(ypart, "rows")
        gram = lax.psum(jnp.dot(ytotal, ytotal.T, precision=lax.Precision.HIGHEST), "params")
        lower = jnp.linalg.cholesky(gram)
        solved = lax.linalg.triangular_solve(lower, ytotal, left_side=True, lower=True)
        basis = (solved * scale).astype(jnp.bfloat16)
    return basis


def solution(mesh):
    placed = (P("rows", "params"), P("rows", "params"), P("rows"), P(), P(None, "params"))
    return jax.shard_map(
        local, mesh=mesh, in_specs=placed, out_specs=P(None, "params"), check_vma=False
    )
```

profile of v0, /device:TPU:0, one launch (start us, length us, event | category | flops | bytes accessed | tf_op | source)
XLA Modules:
  0.0 1694.4 jit_solution(16454283900543719052)
XLA Ops:
  7.3 4.8 copy.24
  12.1 2.1 bitcast_multiply_fusion
  14.3 1.4 convolution_bitcast_fusion
  15.8 162.7 %all-reduce.9.cloned.1.call-done = f32[32,2048]{1,0:T(8,128)} async-done(((f32[32,2048]{1,0:T(8,128)}), f32[32,2048]{1,0:T(8,128)}) %all-reduce.9.cloned.1.call-update) | async-done | bytes 262160 | tf_op jit(solution)/shard_map/psum | solution.py:24
  178.5 2.6 fusion.4
  181.2 170.3 %all-reduce.11.cloned.1.call-done = f32[32,768]{1,0:T(8,128)} async-done(((f32[32,768]{1,0:T(8,128)}), f32[32,768]{1,0:T(8,128)}) %all-reduce.11.cloned.1.call-update) | async-done | bytes 98320 | tf_op jit(solution)/shard_map/psum | solution.py:27
  352.7 79.5 %psum.86 = f32[32,32]{0,1:T(8,128)S(1)} all-reduce(f32[32,32]{0,1:T(8,128)S(1)} %fusion.30), channel_id=1, replica_groups=mesh['rows'=16,'params'=16] {'params'}, use_global_device_ids=true, to_apply=%region_3.0 | all-reduce | flops 1024 | bytes 8192 | tf_op jit(solution)/shard_map/psum | solution.py:28
  432.4 2.9 cholesky.74
  436.6 2.5 custom-call.8
  440.3 1.4 fusion.31
  441.7 152.4 %all-reduce.13.cloned.1.call-done = f32[32,2048]{1,0:T(8,128)} async-done(((f32[32,2048]{1,0:T(8,128)}), f32[32,2048]{1,0:T(8,128)}) %all-reduce.13.cloned.1.call-update) | async-done | bytes 262160 | tf_op jit(solution)/shard_map/psum | solution.py:24
  594.1 2.6 fusion.5
  596.8 170.3 %all-reduce.15.cloned.1.call-done = f32[32,768]{1,0:T(8,128)} async-done(((f32[32,768]{1,0:T(8,128)}), f32[32,768]{1,0:T(8,128)}) %all-reduce.15.cloned.1.call-update) | async-done | bytes 98320 | tf_op jit(solution)/shard_map/psum | solution.py:27
  768.3 79.5 %psum.89 = f32[32,32]{0,1:T(8,128)S(1)} all-reduce(f32[32,32]{0,1:T(8,128)S(1)} %fusion.32), channel_id=1, replica_groups=mesh['rows'=16,'params'=16] {'params'}, use_global_device_ids=true, to_apply=%region_8.11 | all-reduce | flops 1024 | bytes 8192 | tf_op jit(solution)/shard_map/psum | solution.py:28
  847.9 2.9 cholesky.85
  852.2 2.5 custom-call.9
  855.8 1.4 fusion.33
  857.2 152.4 %all-reduce.17.cloned.1.call-done = f32[32,2048]{1,0:T(8,128)} async-done(((f32[32,2048]{1,0:T(8,128)}), f32[32,2048]{1,0:T(8,128)}) %all-reduce.17.cloned.1.call-update) | async-done | bytes 262160 | tf_op jit(solution)/shard_map/psum | solution.py:24
  1009.6 2.6 fusion.6
  1012.3 170.4 %all-reduce.19.cloned.1.call-done = f32[32,768]{1,0:T(8,128)} async-done(((f32[32,768]{1,0:T(8,128)}), f32[32,768]{1,0:T(8,128)}) %all-reduce.19.cloned.1.call-update) | async-done | bytes 98320 | tf_op jit(solution)/shard_map/psum | solution.py:27
  1182.6 1.2 fusion.34
  1183.8 79.5 %psum.92 = f32[32,32]{0,1:T(8,128)S(1)} all-reduce(f32[32,32]{0,1:T(8,128)S(1)} %fusion.34), channel_id=1, replica_groups=mesh['rows'=16,'params'=16] {'params'}, use_global_device_ids=true, to_apply=%region_11.14 | all-reduce | flops 1024 | bytes 8192 | tf_op jit(solution)/shard_map/psum | solution.py:28
  1263.5 2.9 cholesky.96
  1267.7 2.5 custom-call.10
  1271.4 1.4 fusion.35
  1272.8 152.4 %all-reduce.21.cloned.1.call-done = f32[32,2048]{1,0:T(8,128)} async-done(((f32[32,2048]{1,0:T(8,128)}), f32[32,2048]{1,0:T(8,128)}) %all-reduce.21.cloned.1.call-update) | async-done | bytes 262160 | tf_op jit(solution)/shard_map/psum | solution.py:24
  1425.1 2.6 fusion.7
  1427.8 170.4 %all-reduce.23.cloned.1.call-done = f32[32,768]{1,0:T(8,128)} async-done(((f32[32,768]{1,0:T(8,128)}), f32[32,768]{1,0:T(8,128)}) %all-reduce.23.cloned.1.call-update) | async-done | bytes 98320 | tf_op jit(solution)/shard_map/psum | solution.py:27
  1599.4 79.5 %psum.95 = f32[32,32]{0,1:T(8,128)S(1)} all-reduce(f32[32,32]{0,1:T(8,128)S(1)} %fusion.36), channel_id=1, replica_groups=mesh['rows'=16,'params'=16] {'params'}, use_global_device_ids=true, to_apply=%region_14.17 | all-reduce | flops 1024 | bytes 8192 | tf_op jit(solution)/shard_map/psum | solution.py:28
  1679.0 2.9 cholesky.107
  1683.3 2.4 custom-call.11
  1685.7 1.8 fusion.3
  (52 shorter events, 14.0 us)
Async XLA Ops:
  6.5 7.7 copy-start
  6.5 172.0 %all-reduce.9.cloned.1.call-start = ((), (), s32[]{:S(2)}) async-start(), calls=%async_computation | async-start | bytes 524288 | tf_op jit(solution)/shard_map/psum | solution.py:24
  14.2 1.5 copy-start.1
  14.2 1.4 copy-start.2
  15.6 335.9 %all-reduce.11.cloned.1.call-start = ((), (), s32[]{:S(2)}) async-start(), calls=%async_computation.1 | async-start | bytes 196608 | tf_op jit(solution)/shard_map/psum | solution.py:27
  181.2 412.9 %all-reduce.13.cloned.1.call-start = ((), (), s32[]{:S(2)}) async-start(), calls=%async_computation.2 | async-start | bytes 524288 | tf_op jit(solution)/shard_map/psum | solution.py:24
  441.7 325.4 %all-reduce.15.cloned.1.call-start = ((), (), s32[]{:S(2)}) async-start(), calls=%async_computation.3 | async-start | bytes 196608 | tf_op jit(solution)/shard_map/psum | solution.py:27
  596.7 412.9 %all-reduce.17.cloned.1.call-start = ((), (), s32[]{:S(2)}) async-start(), calls=%async_computation.4 | async-start | bytes 524288 | tf_op jit(solution)/shard_map/psum | solution.py:24
  857.2 325.5 %all-reduce.19.cloned.1.call-start = ((), (), s32[]{:S(2)}) async-start(), calls=%async_computation.5 | async-start | bytes 196608 | tf_op jit(solution)/shard_map/psum | solution.py:27
  1012.2 412.9 %all-reduce.21.cloned.1.call-start = ((), (), s32[]{:S(2)}) async-start(), calls=%async_computation.6 | async-start | bytes 524288 | tf_op jit(solution)/shard_map/psum | solution.py:24
  1272.7 325.4 %all-reduce.23.cloned.1.call-start = ((), (), s32[]{:S(2)}) async-start(), calls=%async_computation.7 | async-start | bytes 196608 | tf_op jit(solution)/shard_map/psum | solution.py:27
Sparse Core Ops, SparseCore 0:
  15.8 162.7 all-reduce.8
  181.3 170.2 all-reduce.10
  441.8 152.2 all-reduce.12
  596.8 170.2 all-reduce.14
  857.3 152.2 all-reduce.16
  1012.4 170.2 all-reduce.18
  1272.9 152.2 all-reduce.20
  1427.9 170.2 all-reduce.22
where the time goes:
time: 1700 us; the launch traced here: 1690 us
  waiting for transfers between devices  1300 us (76%)
  blocking collectives  318 us (19%)
  other arithmetic  29.7 us (2%)
  matrix products  26 us (2%)
    psum x4, waiting for transfers between devices, local(): ytotal = lax.psum(ypart, 'rows')  681 us
    psum x4, waiting for transfers between devices, local(): ztotal = lax.psum(zpart, 'params')  620 us
    psum x4, blocking collectives, local(): lax.psum(jnp.dot(ytotal, ytotal.T, precision=lax.Precision.HIGHEST), 'par...  318 us
  transfers between devices with their start and end apart: 8, of which 8 were waited for; matrix products, arithmetic and copies ran while one was open for 0% of the time, Pallas kernels for 0%

commit v1 on v0

--- a/solution.py
+++ b/solution.py
@@ -6,6 +6,11 @@
 
 P_SIZE = 12288
 ITERS = 4
+
+
+def add_all(value, name):
+    blocks = lax.all_gather(value, name)
+    return jnp.sum(blocks, axis=0)
 
 
 def local(jacobian, pattern, row_class, class_weight, probes):
@@ -21,7 +26,7 @@
         zpart = lax.dot_general(
             basis, masked, (((1,), (1,)), ((), ())), preferred_element_type=jnp.float32
         )
-        ztotal = lax.psum(zpart, "params")
+        ztotal = add_all(zpart, "params")
         weighted = (ztotal * weight[None, :]).astype(jnp.bfloat16)
         ypart = jnp.dot(weighted, masked, preferred_element_type=jnp.float32)
         ytotal = lax.psum(ypart, "rows")

time: 1700 us -> 1410 us (0.83)
  waiting for transfers between devices: 1300 us -> 1010 us
    psum x4 -> x0, waiting for transfers between devices: 620 us -> none  [local(): ztotal = lax.psum(zpart, 'params')]
    all_gather x0 -> x4, waiting for transfers between devices: none -> 322 us  [add_all(): blocks = lax.all_gather(value, name)]
where the time goes in v1:
time: 1410 us; the launch traced here: 1400 us
  waiting for transfers between devices  1010 us (72%)
  blocking collectives  318 us (23%)
  other arithmetic  39.4 us (3%)
  matrix products  22.2 us (2%)
    psum x4, waiting for transfers between devices, local(): ytotal = lax.psum(ypart, 'rows')  684 us
    all_gather x4, waiting for transfers between devices, add_all(): blocks = lax.all_gather(value, name)  322 us
    psum x4, blocking collectives, local(): lax.psum(jnp.dot(ytotal, ytotal.T, precision=lax.Precision.HIGHEST), 'par...  318 us
  transfers between devices with their start and end apart: 8, of which 8 were waited for; matrix products, arithmetic and copies ran while one was open for 0% of the time, Pallas kernels for 0%

profile of v1, /device:TPU:0, one launch (start us, length us, event | category | flops | bytes accessed | tf_op | source)
XLA Modules:
  0.0 1404.3 jit_solution(12945017588949257692)
XLA Ops:
  7.3 4.8 copy.24
  12.1 2.1 bitcast_multiply_fusion
  15.8 88.2 %all-gather.9.cloned.1.call-done = f32[512,2048]{1,0:T(8,128)} async-done(((f32[32,2048]{1,0:T(8,128)}), f32[512,2048]{1,0:T(8,128)}) %all-gather.9.cloned.1.call-update) | async-done | bytes 4194320 | tf_op jit(solution)/shard_map/all_gather | solution.py:12
  104.0 2.4 reduce_sum.45
  106.4 1.7 fusion.4
  108.1 170.9 %all-reduce.5.cloned.1.call-done = f32[32,768]{1,0:T(8,128)} async-done(((f32[32,768]{1,0:T(8,128)}), f32[32,768]{1,0:T(8,128)}) %all-reduce.5.cloned.1.call-update) | async-done | bytes 98320 | tf_op jit(solution)/shard_map/psum | solution.py:32
  280.2 79.5 %psum.57 = f32[32,32]{0,1:T(8,128)S(1)} all-reduce(f32[32,32]{0,1:T(8,128)S(1)} %fusion.30), channel_id=1, replica_groups=mesh['rows'=16,'params'=16] {'params'}, use_global_device_ids=true, to_apply=%region_3.0 | all-reduce | flops 1024 | bytes 8192 | tf_op jit(solution)/shard_map/psum | solution.py:33
  359.9 2.9 cholesky.74
  364.1 2.5 custom-call.8
  367.8 1.3 fusion.31
  369.2 77.8 %all-gather.11.cloned.1.call-done = f32[512,2048]{1,0:T(8,128)} async-done(((f32[32,2048]{1,0:T(8,128)}), f32[512,2048]{1,0:T(8,128)}) %all-gather.11.cloned.1.call-update) | async-done | bytes 4194320 | tf_op jit(solution)/shard_map/all_gather | solution.py:12
  447.0 2.4 reduce_sum.47
  449.4 1.7 fusion.5
  451.2 170.9 %all-reduce.7.cloned.1.call-done = f32[32,768]{1,0:T(8,128)} async-done(((f32[32,768]{1,0:T(8,128)}), f32[32,768]{1,0:T(8,128)}) %all-reduce.7.cloned.1.call-update) | async-done | bytes 98320 | tf_op jit(solution)/shard_map/psum | solution.py:32
  623.3 79.5 %psum.59 = f32[32,32]{0,1:T(8,128)S(1)} all-reduce(f32[32,32]{0,1:T(8,128)S(1)} %fusion.32), channel_id=1, replica_groups=mesh['rows'=16,'params'=16] {'params'}, use_global_device_ids=true, to_apply=%region_8.11 | all-reduce | flops 1024 | bytes 8192 | tf_op jit(solution)/shard_map/psum | solution.py:33
  702.9 2.9 cholesky.85
  707.1 2.5 custom-call.9
  712.2 77.8 %all-gather.13.cloned.1.call-done = f32[512,2048]{1,0:T(8,128)} async-done(((f32[32,2048]{1,0:T(8,128)}), f32[512,2048]{1,0:T(8,128)}) %all-gather.13.cloned.1.call-update) | async-done | bytes 4194320 | tf_op jit(solution)/shard_map/all_gather | solution.py:12
  790.0 2.4 reduce_sum.48
  792.4 1.7 fusion.6
  794.2 170.9 %all-reduce.9.cloned.1.call-done = f32[32,768]{1,0:T(8,128)} async-done(((f32[32,768]{1,0:T(8,128)}), f32[32,768]{1,0:T(8,128)}) %all-reduce.9.cloned.1.call-update) | async-done | bytes 98320 | tf_op jit(solution)/shard_map/psum | solution.py:32
  966.3 79.5 %psum.61 = f32[32,32]{0,1:T(8,128)S(1)} all-reduce(f32[32,32]{0,1:T(8,128)S(1)} %fusion.34), channel_id=1, replica_groups=mesh['rows'=16,'params'=16] {'params'}, use_global_device_ids=true, to_apply=%region_11.14 | all-reduce | flops 1024 | bytes 8192 | tf_op jit(solution)/shard_map/psum | solution.py:33
  1045.9 2.9 cholesky.96
  1050.2 2.5 custom-call.10
  1055.2 77.8 %all-gather.15.cloned.1.call-done = f32[512,2048]{1,0:T(8,128)} async-done(((f32[32,2048]{1,0:T(8,128)}), f32[512,2048]{1,0:T(8,128)}) %all-gather.15.cloned.1.call-update) | async-done | bytes 4194320 | tf_op jit(solution)/shard_map/all_gather | solution.py:12
  1133.0 2.4 reduce_sum.49
  1135.5 1.7 fusion.7
  1137.2 171.0 %all-reduce.11.cloned.1.call-done = f32[32,768]{1,0:T(8,128)} async-done(((f32[32,768]{1,0:T(8,128)}), f32[32,768]{1,0:T(8,128)}) %all-reduce.11.cloned.1.call-update) | async-done | bytes 98320 | tf_op jit(solution)/shard_map/psum | solution.py:32
  1309.3 79.5 %psum.63 = f32[32,32]{0,1:T(8,128)S(1)} all-reduce(f32[32,32]{0,1:T(8,128)S(1)} %fusion.36), channel_id=1, replica_groups=mesh['rows'=16,'params'=16] {'params'}, use_global_device_ids=true, to_apply=%region_14.17 | all-reduce | flops 1024 | bytes 8192 | tf_op jit(solution)/shard_map/psum | solution.py:33
  1389.0 2.9 cholesky.107
  1393.2 2.4 custom-call.11
  1395.6 1.8 fusion.3
  (56 shorter events, 19.2 us)
Async XLA Ops:
  6.5 7.7 copy-start
  6.5 97.4 %all-gather.9.cloned.1.call-start = ((), (), s32[]{:S(2)}) async-start(), calls=%async_computation.4 | async-start | bytes 4456448 | tf_op jit(solution)/shard_map/all_gather | solution.py:12
  14.2 1.4 copy-start.1
  14.2 1.4 copy-start.2
  15.6 263.4 %all-reduce.5.cloned.1.call-start = ((), (), s32[]{:S(2)}) async-start(), calls=%async_computation | async-start | bytes 196608 | tf_op jit(solution)/shard_map/psum | solution.py:32
  108.1 338.9 %all-gather.11.cloned.1.call-start = ((), (), s32[]{:S(2)}) async-start(), calls=%async_computation.5 | async-start | bytes 4456448 | tf_op jit(solution)/shard_map/all_gather | solution.py:12
  369.1 252.9 %all-reduce.7.cloned.1.call-start = ((), (), s32[]{:S(2)}) async-start(), calls=%async_computation.1 | async-start | bytes 196608 | tf_op jit(solution)/shard_map/psum | solution.py:32
  451.1 338.9 %all-gather.13.cloned.1.call-start = ((), (), s32[]{:S(2)}) async-start(), calls=%async_computation.6 | async-start | bytes 4456448 | tf_op jit(solution)/shard_map/all_gather | solution.py:12
  712.2 252.9 %all-reduce.9.cloned.1.call-start = ((), (), s32[]{:S(2)}) async-start(), calls=%async_computation.2 | async-start | bytes 196608 | tf_op jit(solution)/shard_map/psum | solution.py:32
  794.1 338.9 %all-gather.15.cloned.1.call-start = ((), (), s32[]{:S(2)}) async-start(), calls=%async_computation.7 | async-start | bytes 4456448 | tf_op jit(solution)/shard_map/all_gather | solution.py:12
  1055.2 252.9 %all-reduce.11.cloned.1.call-start = ((), (), s32[]{:S(2)}) async-start(), calls=%async_computation.3 | async-start | bytes 196608 | tf_op jit(solution)/shard_map/psum | solution.py:32
Sparse Core Ops, SparseCore 0:
  15.7 88.1 all-gather.8
  108.2 170.8 all-reduce.4
  369.2 77.6 all-gather.10
  451.2 170.8 all-reduce.6
  712.3 77.6 all-gather.12
  794.3 170.8 all-reduce.8
  1055.3 77.6 all-gather.14
  1137.3 170.8 all-reduce.10
